TPU v7x, 256 devices: a whole 4x4x8 slice. The times are simulated.
256 devices in a mesh: ctx: 32 (over y, z), uly: 8 (over x, core).
Axes of the slice: x: 4, y: 4, z: 8, core: 2. Of those that a mesh axis runs over, the one named last changes fastest.
Arguments:
- queries: bfloat16 [32768, 32, 128], P(('ctx', 'uly')), may hold values from -20 to 20
- keys: bfloat16 [32768, 8, 128], P(('ctx', 'uly')), may hold values from -20 to 20
- values: bfloat16 [32768, 8, 128], P(('ctx', 'uly')), may hold values from -6 to 6
- grad_out: bfloat16 [32768, 32, 128], P(('ctx', 'uly')), may hold values from -6 to 6
- doc_lengths: int32 [64], replicated, may hold values from 1 to 1024, 32768 in all
Outputs:
- grad_queries: bfloat16 [32768, 32, 128], P(('ctx', 'uly'))
- grad_keys: bfloat16 [32768, 8, 128], P(('ctx', 'uly'))
- grad_values: bfloat16 [32768, 8, 128], P(('ctx', 'uly'))
Inputs may be any that keep to these rules, and one draw needn't show every extreme that they name: `doc_lengths`: positive lengths that sum to 32768; the longest document has exactly 1024 tokens.
All inputs are finite; a program needn't handle non-finite values.
Results may differ from a plain program's by a relative error of at most 0.0069.
Values may be sent and summed in bfloat16 or wider, within the bound.
A program may use at most 64 MiB of HBM per device.

v0:
```python
import jax
import jax.numpy as jnp
from jax import lax
from jax.experimental import pallas as pl
from jax.experimental.pallas import tpu as pltpu
from jax.sharding import PartitionSpec as P

MESH = pl.DeviceIdType.MESH
NT = (((1,), (1,)), ((), ()))
TN = (((0,), (0,)), ((), ()))
LOG2E = 1.4426950408889634

TOK = 128
CHIP = 256
WINDOW = 1280
SPAN = 1152
TILE = 128
ROWS = 256
PAIRS = ROWS // TOK


def kernel(
    heads,
    group,
    chips,
    blocks,
    lengths,
    q_in,
    do_in,
    kv_in,
    dq_out,
    dkv_out,
    kvb,
    qv,
    dov,
    bias,
    s_scr,
    dp_scr,
    dsb,
    acc,
    dqv,
    sbuf,
    rbuf,
    fin,
    kv_loc,
    kv_send,
    kv_recv,
    x_loc,
    x_send,
    x_recv,
    g_send,
    g_recv,
    dq_loc,
    dq_send,
    dq_recv,
    fin_loc,
    fin_send,
    fin_recv,
):
    ctx = lax.axis_index("ctx")
    uly = lax.axis_index("uly")
    x, core = uly // 2, uly % 2
    qheads = heads * group
    scale = TOK**-0.5
    chip = ctx * chips + x
    total = blocks * chips

    def at(chip_number):
        return (chip_number // chips, (chip_number % chips) * 2 + core)

    sibling = (ctx, uly + 1 - 2 * core)
    up = ((ctx + 1) % blocks, uly)
    down = ((ctx + blocks - 1) % blocks, uly)
    right = (ctx, (uly + 2) % (2 * chips))
    left = (ctx, (uly + 2 * chips - 2) % (2 * chips))
    after = at((chip + 1) % total)
    before = at((chip + total - 1) % total)
    onward = at((chip + total + 1 - 2 * core) % total)
    backward = at((chip + total - 1 + 2 * core) % total)

    pos_right = 1024 * (1 - x // (chips - 1))
    pos_left = 1024 * (1 - (x + chips - 2) // (chips - 1))
    pos_mid = 768 - 512 * core

    barrier = pltpu.get_barrier_semaphore()
    for device in (sibling, up, down, right, left, after, before):
        pl.semaphore_signal(barrier, inc=1, device_id=device, device_id_type=MESH)
    pl.semaphore_wait(barrier, 7)

    def remote(src, dst, send, recv, device):
        return pltpu.make_async_remote_copy(
            src_ref=src, dst_ref=dst, send_sem=send, recv_sem=recv, device_id=device, device_id_type=MESH
        )

    def part(h, pos):
        return kvb.at[h, :, pl.ds(pos if isinstance(pos, int) else pl.multiple_of(pos, 256), CHIP), :]

    own_rows = pl.ds(pl.multiple_of(1024 + TOK * core, TOK), TOK)
    other_rows = pl.ds(pl.multiple_of(1024 + TOK * (1 - core), TOK), TOK)

    def kv_local(h):
        return pltpu.make_async_copy(kv_in.at[heads * core + h], kvb.at[h, :, own_rows, :], kv_loc.at[h])

    def kv_swap(h, rows=own_rows):
        return remote(kv_in.at[heads * (1 - core) + h], kvb.at[h, :, rows, :], kv_send.at[h, 0], kv_recv.at[h, 0], sibling)

    def x_local(n, h):
        src, dst = ((q_in, qv), (do_in, dov))[n]
        return pltpu.make_async_copy(
            src.at[pl.ds(qheads * core + group * h, group)], dst.at[core, pl.ds(group * h, group)], x_loc.at[n, h]
        )

    def x_swap(n, h, half=core):
        src, dst = ((q_in, qv), (do_in, dov))[n]
        return remote(
            src.at[pl.ds(qheads * (1 - core) + group * h, group)],
            dst.at[half, pl.ds(group * h, group)],
            x_send.at[n, h],
            x_recv.at[n, h],
            sibling,
        )

    def to_up(h):
        return remote(part(h, 1024), part(h, 0), kv_send.at[h, 4], kv_recv.at[h, 4], up)

    def to_right(h):
        return remote(part(h, pos_right), part(h, 768), kv_send.at[h, 1], kv_recv.at[h, 1], right)

    def to_left(h):
        return remote(part(h, pos_left), part(h, 256), kv_send.at[h, 3], kv_recv.at[h, 3], left)

    def to_onward(h):
        return remote(part(h, pos_mid), part(h, 512), kv_send.at[h, 2], kv_recv.at[h, 2], onward)

    def own_ready(h):
        kv_local(h).wait()
        kv_swap(h, other_rows).wait_recv()
        to_up(h).start()

        @pl.when(x < chips - 1)
        def _():
            to_right(h).start()

        @pl.when(x == 0)
        def _():
            to_left(h).start()

    def far_ready(h):
        to_up(h).wait_recv()

        @pl.when(x == chips - 1)
        def _():
            to_right(h).start()

        @pl.when(x > 0)
        def _():
            to_left(h).start()

    def relay(h):
        @pl.when(core == 0)
        def _():
            to_right(h).wait_recv()

        @pl.when(core == 1)
        def _():
            to_left(h).wait_recv()

        to_onward(h).start()

    def all_ready(h):
        @pl.when(core == 1)
        def _():
            to_right(h).wait_recv()

        @pl.when(core == 0)
        def _():
            to_left(h).wait_recv()

        to_onward(h).wait_recv()
        for n in range(2):
            x_local(n, h).wait()
            x_swap(n, h, 1 - core).wait_recv()

    def back(h, n, device):
        return remote(sbuf.at[h, n], rbuf.at[h, n], g_send.at[h, n], g_recv.at[h, n], device)

    def send_back(h, n, pos, device):
        rows = pl.ds(pos, CHIP)
        sbuf[h, n] = acc[h, :, rows, :].astype(jnp.bfloat16)
        back(h, n, device).start()

    def add_back(h, n, device, pos):
        back(h, n, device).wait_recv()
        rows = pl.ds(pl.multiple_of(pos, 256), CHIP)
        acc[h, :, rows, :] = acc[h, :, rows, :] + rbuf[h, n].astype(jnp.float32)

    def finish_head(h):
        send_back(h, 0, 512, backward)

        @pl.when(core == 0)
        def _():
            send_back(h, 2, 256, right)

        @pl.when(core == 1)
        def _():
            send_back(h, 1, 768, left)

    def second_back(h):
        add_back(h, 0, backward, pos_mid)

        @pl.when(core == 0)
        def _():
            send_back(h, 1, 768, left)

        @pl.when(core == 1)
        def _():
            send_back(h, 2, 256, right)

    def third_back(h):
        add_back(h, 1, left, pos_right)
        add_back(h, 2, right, pos_left)
        send_back(h, 3, 0, down)

    def fin_local(h):
        return pltpu.make_async_copy(
            fin.at[h, :, pl.ds(pl.multiple_of(TOK * core, TOK), TOK), :], dkv_out.at[heads * core + h], fin_loc.at[h]
        )

    def fin_swap(h, owner=core):
        return remote(
            fin.at[h, :, pl.ds(pl.multiple_of(TOK * (1 - core), TOK), TOK), :],
            dkv_out.at[heads * owner + h],
            fin_send.at[h],
            fin_recv.at[h],
            sibling,
        )

    def last_back(h):
        back(h, 3, down).wait_recv()
        rows = pl.ds(1024, CHIP)
        fin[h, 0] = ((acc[h, 0, rows, :] + rbuf[h, 3, 0].astype(jnp.float32)) * scale).astype(jnp.bfloat16)
        fin[h, 1] = (acc[h, 1, rows, :] + rbuf[h, 3, 1].astype(jnp.float32)).astype(jnp.bfloat16)
        fin_local(h).start()
        fin_swap(h).start()

    def dq_slice(h, pair):
        return pl.ds(group * h + PAIRS * pair, PAIRS)

    def dq_local(h, pair):
        return pltpu.make_async_copy(
            dqv.at[core, dq_slice(h, pair)],
            dq_out.at[pl.ds(qheads * core + group * h + PAIRS * pair, PAIRS)],
            dq_loc.at[h, pair],
        )

    def dq_swap(h, pair, owner=core):
        return remote(
            dqv.at[1 - core, dq_slice(h, pair)],
            dq_out.at[pl.ds(qheads * owner + group * h + PAIRS * pair, PAIRS)],
            dq_send.at[h, pair],
            dq_recv.at[h, pair],
            sibling,
        )

    for h in range(heads):
        kv_local(h).start()
        kv_swap(h).start()
    for h in range(heads):
        for n in range(2):
            x_local(n, h).start()
            x_swap(n, h).start()

    for h in range(heads):
        own_ready(h)

    start_pos = chip * CHIP
    token = lax.broadcasted_iota(jnp.int32, (8, CHIP), 1) + start_pos

    def doc(number, carry):
        begin, doc_start = carry
        return begin + lengths[number], jnp.where(token >= begin, begin, doc_start)

    _, doc_start = lax.fori_loop(0, lengths.shape[0], doc, (jnp.int32(0), jnp.zeros((8, CHIP), jnp.int32)))
    for t in range(2):
        low = doc_start[0:1, TOK * t : TOK * (t + 1)] - (start_pos + TOK * t) + 1024
        high = lax.broadcasted_iota(jnp.int32, (1, TOK), 1) + 1024
        for tile in range(SPAN // TILE):
            key = lax.broadcasted_iota(jnp.int32, (TILE, TOK), 0) + tile * TILE
            bias[t, pl.ds(tile * TILE, TILE), :] = jnp.where((key >= low) & (key <= high), 0.0, -1e30)

    far_ready(0)
    for h in range(heads):
        for n in range(2):
            for tile in range(WINDOW // CHIP):
                acc[h, n, pl.ds(tile * CHIP, CHIP), :] = jnp.zeros((CHIP, TOK), jnp.float32)
    far_ready(1)
    relay(0)
    all_ready(0)

    hooks = {
        1: [lambda: relay(1), lambda: far_ready(2)],
        2: [lambda: relay(2), lambda: far_ready(3)],
        3: [lambda: relay(3)],
        4: [lambda: finish_head(0), lambda: all_ready(1)],
        7: [lambda: second_back(0)],
        8: [lambda: finish_head(1), lambda: all_ready(2)],
        10: [lambda: third_back(0)],
        11: [lambda: second_back(1)],
        12: [lambda: finish_head(2), lambda: all_ready(3)],
        13: [lambda: last_back(0)],
        14: [lambda: third_back(1)],
        15: [lambda: second_back(2)],
    }
    pairs = group // PAIRS
    steps = heads * 2 * pairs

    for step in range(steps):
        for each in hooks.get(step, ()):
            each()
        h = step // (2 * pairs)
        t = step // pairs % 2
        pair = step % pairs
        off = t * TOK
        q = qv[t, dq_slice(h, pair)].reshape(ROWS, TOK)
        do = dov[t, dq_slice(h, pair)].reshape(ROWS, TOK)
        tiles = [pl.ds(tile * TILE, TILE) for tile in range(SPAN // TILE)]
        keys = [pl.ds(off + tile * TILE, TILE) for tile in range(SPAN // TILE)]
        top = jnp.full((8, ROWS), -jnp.inf, jnp.float32)
        for tile, key in zip(tiles, keys):
            score = lax.dot_general(kvb[h, 0, key, :], q, NT, preferred_element_type=jnp.float32)
            score = score + jnp.concatenate([bias[t, tile, :]] * PAIRS, axis=1)
            s_scr[tile, :] = score
            dp_scr[tile, :] = lax.dot_general(kvb[h, 1, key, :], do, NT, preferred_element_type=jnp.float32)
            top = jnp.maximum(top, jnp.max(score.reshape(TILE // 8, 8, ROWS), axis=0))
        factor = scale * LOG2E
        shift = jnp.max(top, axis=0, keepdims=True) * factor
        weight = jnp.zeros((8, ROWS), jnp.float32)
        weighted = jnp.zeros((8, ROWS), jnp.float32)
        for tile in tiles:
            expo = jnp.exp2(s_scr[tile, :] * factor - shift)
            s_scr[tile, :] = expo
            weight = weight + jnp.sum(expo.reshape(TILE // 8, 8, ROWS), axis=0)
            weighted = weighted + jnp.sum((expo * dp_scr[tile, :]).reshape(TILE // 8, 8, ROWS), axis=0)
        inverse = 1.0 / jnp.sum(weight, axis=0, keepdims=True)
        delta = jnp.sum(weighted, axis=0, keepdims=True) * inverse
        for tile, key in zip(tiles, keys):
            prob = s_scr[tile, :] * inverse
            dscore = (prob * (dp_scr[tile, :] - delta)).astype(jnp.bfloat16)
            dsb[tile, :] = dscore
            acc[h, 1, key, :] += jnp.dot(prob.astype(jnp.bfloat16), do, preferred_element_type=jnp.float32)
            acc[h, 0, key, :] += jnp.dot(dscore, q, preferred_element_type=jnp.float32)
        dq = lax.dot_general(dsb[...], kvb[h, 0, pl.ds(off, SPAN), :], TN, preferred_element_type=jnp.float32)
        dqv[t, dq_slice(h, pair)] = (dq * scale).astype(jnp.bfloat16).reshape(PAIRS, TOK, TOK)

        @pl.when(core == t)
        def _(h=h, pair=pair):
            dq_local(h, pair).start()

        @pl.when(core == 1 - t)
        def _(h=h, pair=pair):
            dq_swap(h, pair).start()

    finish_head(3)
    last_back(1)
    third_back(2)
    second_back(3)
    last_back(2)
    third_back(3)
    last_back(3)

    for h in range(heads):
        kv_swap(h).wait_send()
        to_up(h).wait_send()
        to_right(h).wait_send()
        to_left(h).wait_send()
        to_onward(h).wait_send()
        for n in range(2):
            x_swap(n, h).wait_send()
        for n, device in enumerate((backward, left, right, down)):
            back(h, n, device).wait_send()
        for pair in range(pairs):
            dq_local(h, pair).wait()
            dq_swap(h, pair).wait_send()
            dq_swap(h, pair, 1 - core).wait_recv()
        fin_local(h).wait()
        fin_swap(h).wait_send()
        fin_swap(h, 1 - core).wait_recv()


def solution(mesh):
    blocks, chips = mesh.shape["ctx"], mesh.shape["uly"] // 2

    def local(queries, keys, values, grad_out, doc_lengths):
        tokens, query_heads, dim = queries.shape
        kv_heads = keys.shape[1]
        heads, group = kv_heads // 2, query_heads // kv_heads
        qheads = heads * group
        pairs = group // PAIRS
        q = jnp.transpose(queries, (1, 0, 2))
        do = jnp.transpose(grad_out, (1, 0, 2))
        kv = jnp.stack([jnp.transpose(keys, (1, 0, 2)), jnp.transpose(values, (1, 0, 2))], axis=1)
        bf16, f32 = jnp.bfloat16, jnp.float32
        vmem, dma = pltpu.VMEM, pltpu.SemaphoreType.DMA
        anywhere = pl.BlockSpec(memory_space=pl.ANY)

        def body(*refs):
            kernel(heads, group, chips, blocks, *refs)

        dq, dkv = pl.pallas_call(
            body,
            out_shape=[
                jax.ShapeDtypeStruct((query_heads, tokens, dim), bf16),
                jax.ShapeDtypeStruct((kv_heads, 2, tokens, dim), bf16),
            ],
            in_specs=[pl.BlockSpec(memory_space=pltpu.SMEM), anywhere, anywhere, anywhere],
            out_specs=[anywhere, anywhere],
            scratch_shapes=[
                vmem((heads, 2, WINDOW, dim), bf16),
                vmem((2, qheads, tokens, dim), bf16),
                vmem((2, qheads, tokens, dim), bf16),
                vmem((2, SPAN, TOK), f32),
                vmem((SPAN, ROWS), f32),
                vmem((SPAN, ROWS), f32),
                vmem((SPAN, ROWS), bf16),
                vmem((heads, 2, WINDOW, dim), f32),
                vmem((2, qheads, tokens, dim), bf16),
                vmem((heads, 4, 2, CHIP, dim), bf16),
                vmem((heads, 4, 2, CHIP, dim), bf16),
                vmem((heads, 2, CHIP, dim), bf16),
                dma((heads,)),
                dma((heads, 5)),
                dma((heads, 5)),
                dma((2, heads)),
                dma((2, heads)),
                dma((2, heads)),
                dma((heads, 4)),
                dma((heads, 4)),
                dma((heads, pairs)),
                dma((heads, pairs)),
                dma((heads, pairs)),
                dma((heads,)),
                dma((heads,)),
                dma((heads,)),
            ],
            compiler_params=pltpu.CompilerParams(
                collective_id=0, has_side_effects=True, vmem_limit_bytes=48 << 20
            ),
        )(doc_lengths, q, do, kv)
        return (
            jnp.transpose(dq, (1, 0, 2)),
            jnp.transpose(dkv[:, 0], (1, 0, 2)),
            jnp.transpose(dkv[:, 1], (1, 0, 2)),
        )

    spread = P(("ctx", "uly"), None, None)
    return jax.shard_map(
        local,
        mesh=mesh,
        in_specs=(spread, spread, spread, spread, P()),
        out_specs=(spread, spread, spread),
        check_vma=False,
    )
```

profile of v0, /device:TPU:1, one launch (start us, length us, event | category | flops | bytes accessed | tf_op | source)
XLA Modules:
  0.0 82.5 jit_solution(12146725129671278981)
XLA Ops:
  0.6 0.0 copy-start.1
  0.6 0.0 copy-start.2
  0.7 1.3 %copy_bitcast_fusion.2 = (bf16[8,1,128,128]{3,2,1,0:T(8,128)(2,1)S(1)}, bf16[8,1,128,128]{3,2,1,0:T(8,128)(2,1)S(1)}) fusion(bf16[128,8,128]{2,1,0:T(8,128)(2,1)} %param.7, bf16[128,8,128]{2,1,0:T(8,128)(2,1)} %param.6), kind=kLoop, calls=%fused_computation.3 | loop fusion | bytes 1048576 | tf_op jit(solution)/shard_map/stack | solution.py:401
  1.9 0.1 pad_maximum_fusion.refs_3_
  2.0 0.0 copy-done.1
  2.0 0.3 copy-done.2
  2.3 0.8 copy_bitcast_fusion
  3.1 0.0 copy-start
  3.2 0.6 copy-done
  3.8 75.3 %shard_map.76 = (bf16[32,128,128]{2,1,0:T(8,128)(2,1)S(1)}, bf16[8,2,128,128]{3,2,1,0:T(8,128)(2,1)S(1)}) custom-call(s32[64]{0:T(128)S(1)} %copy-done, bf16[32,128,128]{2,1,0:T(8,128)(2,1)S(1)} %get-tuple-element.15.refs_1_, bf16[32,128,128]{2,1,0:T(8,128)(2,1)S(1)} %get-tuple-element.14.refs_2_, bf16[8,2,128,128]{3,2,1,0:T(8,128)(2,1)S(1)} %pad_maximum_fusion.refs_3_), custom_call_target="tpu_custom_call" | custom-call | tf_op jit(solution)/shard_map/pallas_call | solution.py:409
  79.1 1.6 %copy.12 = bf16[128,32,128]{2,1,0:T(8,128)(2,1)} copy(bf16[128,32,128]{2,0,1:T(8,128)(2,1)S(1)} %bitcast.21) | data formatting | bytes 2097152
  80.8 0.9 %copy.14 = bf16[128,8,128]{2,1,0:T(8,128)(2,1)} copy(bf16[128,8,128]{2,0,1:T(8,128)(2,1)S(1)} %get-tuple-element.10) | data formatting | bytes 524288
  81.6 0.9 %copy.13 = bf16[128,8,128]{2,1,0:T(8,128)(2,1)} copy(bf16[128,8,128]{2,0,1:T(8,128)(2,1)S(1)} %get-tuple-element.11) | data formatting | bytes 524288
  (1 shorter events, 0.0 us)
Async XLA Ops:
  0.6 1.4 %copy-start.1 = (bf16[128,32,128]{2,1,0:T(8,128)(2,1)S(1)}, bf16[128,32,128]{2,1,0:T(8,128)(2,1)}, u32[]{:S(2)}) copy-start(bf16[128,32,128]{2,1,0:T(8,128)(2,1)} %param.8) | copy-start | bytes 3145732
  0.6 1.7 %copy-start.2 = (bf16[128,32,128]{2,1,0:T(8,128)(2,1)S(1)}, bf16[128,32,128]{2,1,0:T(8,128)(2,1)}, u32[]{:S(2)}) copy-start(bf16[128,32,128]{2,1,0:T(8,128)(2,1)} %param.5) | copy-start | bytes 3145732
  3.1 0.7 copy-start
where the time goes:
time: 82.6 us; the launch traced here: 82.5 us
  Pallas kernels  75.3 us (91%)
  local copies, waits for them, and re-layouts  6.51 us (8%)
    pallas_call x1, Pallas kernels, local(): pl.pallas_call(body, out_shape=[jax.ShapeDtypeStruct((query_heads, tokens...  75.3 us
    unnamed x9, local copies, waits for them, and re-layouts  4.4 us

commit v1 on v0

v1 whole, which is shorter than its diff:
```python
import jax
import jax.numpy as jnp
from jax import lax
from jax.experimental import pallas as pl
from jax.experimental.pallas import tpu as pltpu
from jax.sharding import PartitionSpec as P

MESH = pl.DeviceIdType.MESH
NT = (((1,), (1,)), ((), ()))
TN = (((0,), (0,)), ((), ()))
LOG2E = 1.4426950408889634

TOK = 128
CHIP = 256
WINDOW = 1280
SPAN = 1152
TILE = 128
ROWS = 256
PAIRS = ROWS // TOK


def kernel(
    heads,
    group,
    chips,
    blocks,
    lengths,
    q_in,
    do_in,
    kv_in,
    dq_out,
    dkv_out,
    kvb,
    qv,
    dov,
    bias,
    s_scr,
    dp_scr,
    dsb,
    acc,
    dqv,
    sbuf,
    rbuf,
    fin,
    swap_send,
    swap_recv,
    kv_send,
    kv_recv,
    x_send,
    x_recv,
    g_send,
    g_recv,
    dq_send,
    dq_recv,
    fin_send,
    fin_recv,
):
    ctx = lax.axis_index("ctx")
    uly = lax.axis_index("uly")
    x, core = uly // 2, uly % 2
    qheads = heads * group
    scale = TOK**-0.5
    chip = ctx * chips + x
    total = blocks * chips
    pairs = group // PAIRS
    steps = heads * 2 * pairs

    def at(block, place, its_core):
        return (block % blocks, (place % chips) * 2 + its_core)

    def device(number):
        number = (number + total) % total
        return (number // chips, (number % chips) * 2 + core)

    sibling = (ctx, uly + 1 - 2 * core)

    def up(its_core=core):
        return at(ctx + 1, x, its_core)

    def down(its_core=core):
        return at(ctx + blocks - 1, x, its_core)

    def right(its_core=core):
        return at(ctx, x + 1, its_core)

    def left(its_core=core):
        return at(ctx, x + chips - 1, its_core)

    onward = device(chip + 1 - 2 * core)
    backward = device(chip - 1 + 2 * core)

    pos_right = 1024 * (1 - x // (chips - 1))
    pos_left = 1024 * (1 - (x + chips - 2) // (chips - 1))
    pos_mid = 768 - 512 * core

    barrier = pltpu.get_barrier_semaphore()
    partners = [sibling, onward, backward]
    for its_core in (0, 1):
        partners += [up(its_core), down(its_core), right(its_core), left(its_core)]
    for each in partners:
        pl.semaphore_signal(barrier, inc=1, device_id=each, device_id_type=MESH)
    pl.semaphore_wait(barrier, len(partners))

    def remote(src, dst, send, recv, target):
        return pltpu.make_async_remote_copy(
            src_ref=src, dst_ref=dst, send_sem=send, recv_sem=recv, device_id=target, device_id_type=MESH
        )

    def rows_at(pos, half):
        start = pos + TOK * half
        return pl.ds(start if isinstance(start, int) else pl.multiple_of(start, TOK), TOK)

    def swap(h, half=core):
        return remote(
            kv_in.at[heads * (1 - core) + h],
            kvb.at[h, :, rows_at(1024, half), :],
            swap_send.at[h],
            swap_recv.at[h],
            sibling,
        )

    def x_swap(n, h, half=core):
        src, dst = ((q_in, qv), (do_in, dov))[n]
        return remote(
            src.at[pl.ds(qheads * (1 - core) + group * h, group)],
            dst.at[half, pl.ds(group * h, group)],
            x_send.at[n, h],
            x_recv.at[n, h],
            sibling,
        )

    def send_own(h, slot, target):
        for j in (0, 1):
            remote(
                kv_in.at[heads * j + h],
                kvb.at[h, :, rows_at(1024 - 256 * slot, core), :],
                kv_send.at[h, slot - 1, j],
                kv_recv.at[h, slot - 1, core],
                target(j),
            ).start()

    def forward(h, slot, pos, half, target):
        return remote(
            kvb.at[h, :, rows_at(pos, half), :],
            kvb.at[h, :, rows_at(1024 - 256 * slot, half), :],
            kv_send.at[h, slot - 1, half],
            kv_recv.at[h, slot - 1, half],
            target,
        )

    def own_send(h):
        send_own(h, 4, up)

        @pl.when(x < chips - 1)
        def _():
            send_own(h, 1, right)

        @pl.when(x == 0)
        def _():
            send_own(h, 3, left)

    def far_ready(h):
        for half in (0, 1):
            forward(h, 4, 1024, half, up()).wait_recv()

            @pl.when(x == chips - 1)
            def _():
                forward(h, 1, 0, half, right()).start()

            @pl.when(x > 0)
            def _():
                forward(h, 3, 0, half, left()).start()

    def relay(h):
        for half in (0, 1):

            @pl.when(core == 0)
            def _():
                forward(h, 1, 0, half, right()).wait_recv()

            @pl.when(core == 1)
            def _():
                forward(h, 3, 0, half, left()).wait_recv()

            forward(h, 2, pos_mid, half, onward).start()

    def all_ready(h):
        for half in (0, 1):

            @pl.when(core == 1)
            def _():
                forward(h, 1, 0, half, right()).wait_recv()

            @pl.when(core == 0)
            def _():
                forward(h, 3, 0, half, left()).wait_recv()

            forward(h, 2, 0, half, onward).wait_recv()
        swap(h, 1 - core).wait_recv()
        for n in range(2):
            x_swap(n, h, 1 - core).wait_recv()

    def back(h, n, i, target):
        return remote(sbuf.at[h, n, i], rbuf.at[h, n, i], g_send.at[h, n, i], g_recv.at[h, n, i], target)

    def send_back(h, n, i, pos, target):
        sbuf[h, n, i] = acc[h, i, pl.ds(pos, CHIP), :].astype(jnp.bfloat16)
        back(h, n, i, target).start()

    def add_back(h, n, i, target, pos):
        back(h, n, i, target).wait_recv()
        rows = pl.ds(pl.multiple_of(pos, 256), CHIP)
        acc[h, i, rows, :] = acc[h, i, rows, :] + rbuf[h, n, i].astype(jnp.float32)

    def finish_head(h):
        for i in range(2):
            send_back(h, 0, i, 512, backward)

            @pl.when(core == 0)
            def _():
                send_back(h, 2, i, 256, right())

            @pl.when(core == 1)
            def _():
                send_back(h, 1, i, 768, left())

    def second_back(h):
        for i in range(2):
            add_back(h, 0, i, backward, pos_mid)

            @pl.when(core == 0)
            def _():
                send_back(h, 1, i, 768, left())

            @pl.when(core == 1)
            def _():
                send_back(h, 2, i, 256, right())

    def third_back(h):
        for i in range(2):
            add_back(h, 1, i, left(), pos_right)
            add_back(h, 2, i, right(), pos_left)
            send_back(h, 3, i, 0, down())

    def fin_swap(h, i, owner=core):
        return remote(fin.at[h, i], dkv_out.at[heads * owner + h, i], fin_send.at[h, i], fin_recv.at[h, i], sibling)

    def last_back(h):
        for i in range(2):
            back(h, 3, i, down()).wait_recv()
            whole = acc[h, i, pl.ds(1024, CHIP), :] + rbuf[h, 3, i].astype(jnp.float32)
            if i == 0:
                whole = whole * scale
            whole = whole.astype(jnp.bfloat16)
            for k in (0, 1):

                @pl.when(core == k)
                def _():
                    dkv_out[heads * k + h, i] = whole[TOK * k : TOK * (k + 1)]
                    fin[h, i] = whole[TOK * (1 - k) : TOK * (2 - k)]

            fin_swap(h, i).start()

    def dq_swap(h, pair, owner=core):
        return remote(
            dqv.at[pl.ds(group * h + PAIRS * pair, PAIRS)],
            dq_out.at[pl.ds(qheads * owner + group * h + PAIRS * pair, PAIRS)],
            dq_send.at[h, pair],
            dq_recv.at[h, pair],
            sibling,
        )

    for h in range(heads):
        own_send(h)
        swap(h).start()
        for n in range(2):
            x_swap(n, h).start()
    for k in (0, 1):

        @pl.when(core == k)
        def _():
            for h in range(heads):
                kvb[h, :, pl.ds(1024 + TOK * k, TOK), :] = kv_in[heads * k + h]
            for head in range(qheads):
                qv[k, head] = q_in[qheads * k + head]
                dov[k, head] = do_in[qheads * k + head]

    start_pos = chip * CHIP
    token = lax.broadcasted_iota(jnp.int32, (8, CHIP), 1) + start_pos

    def doc(number, carry):
        begin, doc_start = carry
        return begin + lengths[number], jnp.where(token >= begin, begin, doc_start)

    _, doc_start = lax.fori_loop(0, lengths.shape[0], doc, (jnp.int32(0), jnp.zeros((8, CHIP), jnp.int32)))
    for t in range(2):
        low = doc_start[0:1, TOK * t : TOK * (t + 1)] - (start_pos + TOK * t) + 1024
        high = lax.broadcasted_iota(jnp.int32, (1, TOK), 1) + 1024
        for tile in range(SPAN // TILE):
            key = lax.broadcasted_iota(jnp.int32, (TILE, TOK), 0) + tile * TILE
            bias[t, pl.ds(tile * TILE, TILE), :] = jnp.where((key >= low) & (key <= high), 0.0, -1e30)

    far_ready(0)
    for h in range(heads):
        for n in range(2):
            for tile in range(WINDOW // CHIP):
                acc[h, n, pl.ds(tile * CHIP, CHIP), :] = jnp.zeros((CHIP, TOK), jnp.float32)
    far_ready(1)
    relay(0)
    all_ready(0)

    hooks = {
        1: [lambda: relay(1), lambda: far_ready(2)],
        2: [lambda: relay(2), lambda: far_ready(3)],
        3: [lambda: relay(3)],
        4: [lambda: finish_head(0), lambda: all_ready(1)],
        7: [lambda: second_back(0)],
        8: [lambda: finish_head(1), lambda: all_ready(2)],
        10: [lambda: third_back(0)],
        11: [lambda: second_back(1)],
        12: [lambda: finish_head(2), lambda: all_ready(3)],
        13: [lambda: last_back(0)],
        14: [lambda: third_back(1)],
        15: [lambda: second_back(2)],
    }

    for step in range(steps):
        for each in hooks.get(step, ()):
            each()
        h = step // (2 * pairs)
        t = step // pairs % 2
        pair = step % pairs
        off = t * TOK
        mine = pl.ds(group * h + PAIRS * pair, PAIRS)
        q = qv[t, mine].reshape(ROWS, TOK)
        do = dov[t, mine].reshape(ROWS, TOK)
        tiles = [pl.ds(tile * TILE, TILE) for tile in range(SPAN // TILE)]
        keys = [pl.ds(off + tile * TILE, TILE) for tile in range(SPAN // TILE)]
        top = jnp.full((8, ROWS), -jnp.inf, jnp.float32)
        for tile, key in zip(tiles, keys):
            score = lax.dot_general(kvb[h, 0, key, :], q, NT, preferred_element_type=jnp.float32)
            score = score + jnp.concatenate([bias[t, tile, :]] * PAIRS, axis=1)
            s_scr[tile, :] = score
            dp_scr[tile, :] = lax.dot_general(kvb[h, 1, key, :], do, NT, preferred_element_type=jnp.float32)
            top = jnp.maximum(top, jnp.max(score.reshape(TILE // 8, 8, ROWS), axis=0))
        factor = scale * LOG2E
        shift = jnp.max(top, axis=0, keepdims=True) * factor
        weight = jnp.zeros((8, ROWS), jnp.float32)
        weighted = jnp.zeros((8, ROWS), jnp.float32)
        for tile in tiles:
            expo = jnp.exp2(s_scr[tile, :] * factor - shift)
            s_scr[tile, :] = expo
            weight = weight + jnp.sum(expo.reshape(TILE // 8, 8, ROWS), axis=0)
            weighted = weighted + jnp.sum((expo * dp_scr[tile, :]).reshape(TILE // 8, 8, ROWS), axis=0)
        inverse = 1.0 / jnp.sum(weight, axis=0, keepdims=True)
        delta = jnp.sum(weighted, axis=0, keepdims=True) * inverse
        for tile, key in zip(tiles, keys):
            prob = s_scr[tile, :] * inverse
            dscore = (prob * (dp_scr[tile, :] - delta)).astype(jnp.bfloat16)
            dsb[tile, :] = dscore
            acc[h, 1, key, :] += jnp.dot(prob.astype(jnp.bfloat16), do, preferred_element_type=jnp.float32)
            acc[h, 0, key, :] += jnp.dot(dscore, q, preferred_element_type=jnp.float32)
        dq = lax.dot_general(dsb[...], kvb[h, 0, pl.ds(off, SPAN), :], TN, preferred_element_type=jnp.float32)
        dq = (dq * scale).astype(jnp.bfloat16).reshape(PAIRS, TOK, TOK)

        @pl.when(core == t)
        def _():
            dq_out[pl.ds(qheads * t + group * h + PAIRS * pair, PAIRS)] = dq

        @pl.when(core == 1 - t)
        def _():
            dqv[mine] = dq
            dq_swap(h, pair).start()

    finish_head(3)
    last_back(1)
    third_back(2)
    second_back(3)
    last_back(2)
    third_back(3)
    last_back(3)

    for h in range(heads):
        swap(h).wait_send()
        for slot, target in ((1, right()), (2, onward), (3, left()), (4, up())):
            for half in (0, 1):
                forward(h, slot, 0, half, target).wait_send()
        for n in range(2):
            x_swap(n, h).wait_send()
        for i in range(2):
            for n, target in enumerate((backward, left(), right(), down())):
                back(h, n, i, target).wait_send()
            fin_swap(h, i).wait_send()
            fin_swap(h, i, 1 - core).wait_recv()
        for pair in range(pairs):
            dq_swap(h, pair).wait_send()
            dq_swap(h, pair, 1 - core).wait_recv()


def solution(mesh):
    blocks, chips = mesh.shape["ctx"], mesh.shape["uly"] // 2

    def local(queries, keys, values, grad_out, doc_lengths):
        tokens, query_heads, dim = queries.shape
        kv_heads = keys.shape[1]
        heads, group = kv_heads // 2, query_heads // kv_heads
        qheads = heads * group
        pairs = group // PAIRS
        q = jnp.transpose(queries, (1, 0, 2))
        do = jnp.transpose(grad_out, (1, 0, 2))
        kv = jnp.stack([jnp.transpose(keys, (1, 0, 2)), jnp.transpose(values, (1, 0, 2))], axis=1)
        bf16, f32 = jnp.bfloat16, jnp.float32
        vmem, dma = pltpu.VMEM, pltpu.SemaphoreType.DMA
        inside = pl.BlockSpec(memory_space=pltpu.VMEM)

        def body(*refs):
            kernel(heads, group, chips, blocks, *refs)

        dq, dkv = pl.pallas_call(
            body,
            out_shape=[
                jax.ShapeDtypeStruct((query_heads, tokens, dim), bf16),
                jax.ShapeDtypeStruct((kv_heads, 2, tokens, dim), bf16),
            ],
            in_specs=[pl.BlockSpec(memory_space=pltpu.SMEM), inside, inside, inside],
            out_specs=[inside, inside],
            scratch_shapes=[
                vmem((heads, 2, WINDOW, dim), bf16),
                vmem((2, qheads, tokens, dim), bf16),
                vmem((2, qheads, tokens, dim), bf16),
                vmem((2, SPAN, TOK), f32),
                vmem((SPAN, ROWS), f32),
                vmem((SPAN, ROWS), f32),
                vmem((SPAN, ROWS), bf16),
                vmem((heads, 2, WINDOW, dim), f32),
                vmem((qheads, tokens, dim), bf16),
                vmem((heads, 4, 2, CHIP, dim), bf16),
                vmem((heads, 4, 2, CHIP, dim), bf16),
                vmem((heads, 2, TOK, dim), bf16),
                dma((heads,)),
                dma((heads,)),
                dma((heads, 4, 2)),
                dma((heads, 4, 2)),
                dma((2, heads)),
                dma((2, heads)),
                dma((heads, 4, 2)),
                dma((heads, 4, 2)),
                dma((heads, pairs)),
                dma((heads, pairs)),
                dma((heads, 2)),
                dma((heads, 2)),
            ],
            compiler_params=pltpu.CompilerParams(
                collective_id=0, has_side_effects=True, vmem_limit_bytes=48 << 20
            ),
        )(doc_lengths, q, do, kv)
        return (
            jnp.transpose(dq, (1, 0, 2)),
            jnp.transpose(dkv[:, 0], (1, 0, 2)),
            jnp.transpose(dkv[:, 1], (1, 0, 2)),
        )

    spread = P(("ctx", "uly"), None, None)
    return jax.shard_map(
        local,
        mesh=mesh,
        in_specs=(spread, spread, spread, spread, P()),
        out_specs=(spread, spread, spread),
        check_vma=False,
    )
```

time: 82.6 us -> 80.4 us (0.973)
  Pallas kernels: 75.3 us -> 72.8 us
    pallas_call x1, Pallas kernels: 75.3 us -> 72.8 us  [local(): pl.pallas_call(body, out_shape=[jax.ShapeDtypeStruct((query_heads, tokens...]
where the time goes in v1:
time: 80.4 us; the launch traced here: 80 us
  Pallas kernels  72.8 us (91%)
  local copies, waits for them, and re-layouts  6.51 us (8%)
    pallas_call x1, Pallas kernels, local(): pl.pallas_call(body, out_shape=[jax.ShapeDtypeStruct((query_heads, tokens...  72.8 us
    unnamed x9, local copies, waits for them, and re-layouts  4.4 us

profile of v1, /device:TPU:1, one launch (start us, length us, event | category | flops | bytes accessed | tf_op | source)
XLA Modules:
  0.0 80.0 jit_solution(17774458963867211930)
XLA Ops:
  0.6 0.0 copy-start.1
  0.6 0.0 copy-start.2
  0.7 1.3 %copy_bitcast_fusion.2 = (bf16[8,1,128,128]{3,2,1,0:T(8,128)(2,1)S(1)}, bf16[8,1,128,128]{3,2,1,0:T(8,128)(2,1)S(1)}) fusion(bf16[128,8,128]{2,1,0:T(8,128)(2,1)} %param.7, bf16[128,8,128]{2,1,0:T(8,128)(2,1)} %param.6), kind=kLoop, calls=%fused_computation.3 | loop fusion | bytes 1048576 | tf_op jit(solution)/shard_map/stack | solution.py:411
  1.9 0.1 pad_maximum_fusion.refs_3_
  2.0 0.0 copy-done.1
  2.0 0.3 copy-done.2
  2.3 0.8 %copy_bitcast_fusion = (bf16[32,128,128]{2,1,0:T(8,128)(2,1)S(1)}, bf16[32,128,128]{2,1,0:T(8,128)(2,1)S(1)}) fusion(bf16[128,32,128]{2,1,0:T(8,128)(2,1)S(1)} %copy-done.1, bf16[128,32,128]{2,1,0:T(8,128)(2,1)S(1)} %copy-done.2), kind=kLoop, calls=%fused_computation | loop fusion | bytes 4194304 | tf_op jit(solution)/shard_map/transpose | solution.py:410
  3.1 0.0 copy-start
  3.2 0.6 copy-done
  3.8 72.8 %shard_map.76 = (bf16[32,128,128]{2,1,0:T(8,128)(2,1)S(1)}, bf16[8,2,128,128]{3,2,1,0:T(8,128)(2,1)S(1)}) custom-call(s32[64]{0:T(128)S(1)} %copy-done, bf16[32,128,128]{2,1,0:T(8,128)(2,1)S(1)} %get-tuple-element.15.refs_1_, bf16[32,128,128]{2,1,0:T(8,128)(2,1)S(1)} %get-tuple-element.14.refs_2_, bf16[8,2,128,128]{3,2,1,0:T(8,128)(2,1)S(1)} %pad_maximum_fusion.refs_3_), custom_call_target="tpu_custom_call" | custom-call | tf_op jit(solution)/shard_map/pallas_call | solution.py:419
  76.6 1.6 %copy.12 = bf16[128,32,128]{2,1,0:T(8,128)(2,1)} copy(bf16[128,32,128]{2,0,1:T(8,128)(2,1)S(1)} %bitcast.21) | data formatting | bytes 2097152
  78.3 0.9 %copy.14 = bf16[128,8,128]{2,1,0:T(8,128)(2,1)} copy(bf16[128,8,128]{2,0,1:T(8,128)(2,1)S(1)} %get-tuple-element.10) | data formatting | bytes 524288
  79.2 0.9 %copy.13 = bf16[128,8,128]{2,1,0:T(8,128)(2,1)} copy(bf16[128,8,128]{2,0,1:T(8,128)(2,1)S(1)} %get-tuple-element.11) | data formatting | bytes 524288
  (1 shorter events, 0.0 us)
Async XLA Ops:
  0.6 1.4 %copy-start.1 = (bf16[128,32,128]{2,1,0:T(8,128)(2,1)S(1)}, bf16[128,32,128]{2,1,0:T(8,128)(2,1)}, u32[]{:S(2)}) copy-start(bf16[128,32,128]{2,1,0:T(8,128)(2,1)} %param.8) | copy-start | bytes 3145732
  0.6 1.7 %copy-start.2 = (bf16[128,32,128]{2,1,0:T(8,128)(2,1)S(1)}, bf16[128,32,128]{2,1,0:T(8,128)(2,1)}, u32[]{:S(2)}) copy-start(bf16[128,32,128]{2,1,0:T(8,128)(2,1)} %param.5) | copy-start | bytes 3145732
  3.1 0.7 copy-start

commit v2 on v1

--- a/solution.py
+++ b/solution.py
@@ -24,12 +24,23 @@
     group,
     chips,
     blocks,
-    lengths,
+    lengths_in,
     q_in,
     do_in,
-    kv_in,
+    k_in,
+    v_in,
     dq_out,
-    dkv_out,
+    dk_out,
+    dv_out,
+    lengths,
+    q_raw,
+    do_raw,
+    kv_raw,
+    kv_own,
+    q_swap,
+    do_swap,
+    dqh,
+    dkvh,
     kvb,
     qv,
     dov,
@@ -54,6 +65,7 @@
     dq_recv,
     fin_send,
     fin_recv,
+    in_sem,
 ):
     ctx = lax.axis_index("ctx")
     uly = lax.axis_index("uly")
@@ -93,6 +105,15 @@
     pos_left = 1024 * (1 - (x + chips - 2) // (chips - 1))
     pos_mid = 768 - 512 * core
 
+    sources = (k_in, v_in, q_in, do_in, lengths_in)
+    places = (kv_raw.at[0], kv_raw.at[1], q_raw, do_raw, lengths)
+    loads = [pltpu.make_async_copy(src, dst, in_sem.at[n]) for n, (src, dst) in enumerate(zip(sources, places))]
+    for load in loads:
+        load.start()
+    for n in range(2):
+        loads[n].wait()
+        kv_own[n] = jnp.transpose(kv_raw[n], (1, 0, 2))
+
     barrier = pltpu.get_barrier_semaphore()
     partners = [sibling, onward, backward]
     for its_core in (0, 1):
@@ -112,7 +133,7 @@
 
     def swap(h, half=core):
         return remote(
-            kv_in.at[heads * (1 - core) + h],
+            kv_own.at[:, heads * (1 - core) + h],
             kvb.at[h, :, rows_at(1024, half), :],
             swap_send.at[h],
             swap_recv.at[h],
@@ -120,9 +141,9 @@
         )
 
     def x_swap(n, h, half=core):
-        src, dst = ((q_in, qv), (do_in, dov))[n]
+        src, dst = ((q_swap, qv), (do_swap, dov))[n]
         return remote(
-            src.at[pl.ds(qheads * (1 - core) + group * h, group)],
+            src.at[pl.ds(group * h, group)],
             dst.at[half, pl.ds(group * h, group)],
             x_send.at[n, h],
             x_recv.at[n, h],
@@ -132,7 +153,7 @@
     def send_own(h, slot, target):
         for j in (0, 1):
             remote(
-                kv_in.at[heads * j + h],
+                kv_own.at[:, heads * j + h],
                 kvb.at[h, :, rows_at(1024 - 256 * slot, core), :],
                 kv_send.at[h, slot - 1, j],
                 kv_recv.at[h, slot - 1, core],
@@ -149,8 +170,6 @@
         )
 
     def own_send(h):
-        send_own(h, 4, up)
-
         @pl.when(x < chips - 1)
         def _():
             send_own(h, 1, right)
@@ -243,7 +262,7 @@
             send_back(h, 3, i, 0, down())
 
     def fin_swap(h, i, owner=core):
-        return remote(fin.at[h, i], dkv_out.at[heads * owner + h, i], fin_send.at[h, i], fin_recv.at[h, i], sibling)
+        return remote(fin.at[h, i], dkvh.at[i, heads * owner + h], fin_send.at[h, i], fin_recv.at[h, i], sibling)
 
     def last_back(h):
         for i in range(2):
@@ -256,7 +275,7 @@
 
                 @pl.when(core == k)
                 def _():
-                    dkv_out[heads * k + h, i] = whole[TOK * k : TOK * (k + 1)]
+                    dkvh[i, heads * k + h] = whole[TOK * k : TOK * (k + 1)]
                     fin[h, i] = whole[TOK * (1 - k) : TOK * (2 - k)]
 
             fin_swap(h, i).start()
@@ -264,27 +283,42 @@
     def dq_swap(h, pair, owner=core):
         return remote(
             dqv.at[pl.ds(group * h + PAIRS * pair, PAIRS)],
-            dq_out.at[pl.ds(qheads * owner + group * h + PAIRS * pair, PAIRS)],
+            dqh.at[pl.ds(qheads * owner + group * h + PAIRS * pair, PAIRS)],
             dq_send.at[h, pair],
             dq_recv.at[h, pair],
             sibling,
         )
 
     for h in range(heads):
-        own_send(h)
+        send_own(h, 4, up)
+        if h < 2:
+            own_send(h)
         swap(h).start()
+    loads[2].wait()
+    loads[3].wait()
+    for k in (0, 1):
+
+        @pl.when(core == k)
+        def _():
+            other = pl.ds(qheads * (1 - k), qheads)
+            q_swap[...] = jnp.transpose(q_raw[:, other, :], (1, 0, 2))
+            do_swap[...] = jnp.transpose(do_raw[:, other, :], (1, 0, 2))
+
+    for h in range(heads):
         for n in range(2):
             x_swap(n, h).start()
+    far_ready(0)
     for k in (0, 1):
 
         @pl.when(core == k)
         def _():
+            mine = pl.ds(qheads * k, qheads)
+            qv[k] = jnp.transpose(q_raw[:, mine, :], (1, 0, 2))
+            dov[k] = jnp.transpose(do_raw[:, mine, :], (1, 0, 2))
             for h in range(heads):
-                kvb[h, :, pl.ds(1024 + TOK * k, TOK), :] = kv_in[heads * k + h]
-            for head in range(qheads):
-                qv[k, head] = q_in[qheads * k + head]
-                dov[k, head] = do_in[qheads * k + head]
-
+                kvb[h, :, pl.ds(1024 + TOK * k, TOK), :] = kv_own[:, heads * k + h]
+
+    loads[4].wait()
     start_pos = chip * CHIP
     token = lax.broadcasted_iota(jnp.int32, (8, CHIP), 1) + start_pos
 
@@ -300,20 +334,21 @@
             key = lax.broadcasted_iota(jnp.int32, (TILE, TOK), 0) + tile * TILE
             bias[t, pl.ds(tile * TILE, TILE), :] = jnp.where((key >= low) & (key <= high), 0.0, -1e30)
 
-    far_ready(0)
     for h in range(heads):
         for n in range(2):
             for tile in range(WINDOW // CHIP):
                 acc[h, n, pl.ds(tile * CHIP, CHIP), :] = jnp.zeros((CHIP, TOK), jnp.float32)
+    relay(0)
+    own_send(2)
     far_ready(1)
-    relay(0)
     all_ready(0)
 
     hooks = {
-        1: [lambda: relay(1), lambda: far_ready(2)],
-        2: [lambda: relay(2), lambda: far_ready(3)],
-        3: [lambda: relay(3)],
+        1: [lambda: relay(1), lambda: own_send(3), lambda: far_ready(2)],
+        2: [lambda: far_ready(3)],
+        3: [lambda: relay(2)],
         4: [lambda: finish_head(0), lambda: all_ready(1)],
+        5: [lambda: relay(3)],
         7: [lambda: second_back(0)],
         8: [lambda: finish_head(1), lambda: all_ready(2)],
         10: [lambda: third_back(0)],
@@ -365,7 +400,7 @@
 
         @pl.when(core == t)
         def _():
-            dq_out[pl.ds(qheads * t + group * h + PAIRS * pair, PAIRS)] = dq
+            dqh[pl.ds(qheads * t + group * h + PAIRS * pair, PAIRS)] = dq
 
         @pl.when(core == 1 - t)
         def _():
@@ -375,6 +410,13 @@
     finish_head(3)
     last_back(1)
     third_back(2)
+    for h in range(heads):
+        for pair in range(pairs):
+            dq_swap(h, pair).wait_send()
+            dq_swap(h, pair, 1 - core).wait_recv()
+    for k in (0, 1):
+        some = pl.ds(qheads * k, qheads)
+        dq_out[:, some, :] = jnp.transpose(dqh[some], (1, 0, 2))
     second_back(3)
     last_back(2)
     third_back(3)
@@ -392,9 +434,8 @@
                 back(h, n, i, target).wait_send()
             fin_swap(h, i).wait_send()
             fin_swap(h, i, 1 - core).wait_recv()
-        for pair in range(pairs):
-            dq_swap(h, pair).wait_send()
-            dq_swap(h, pair, 1 - core).wait_recv()
+    dk_out[...] = jnp.transpose(dkvh[0], (1, 0, 2))
+    dv_out[...] = jnp.transpose(dkvh[1], (1, 0, 2))
 
 
 def solution(mesh):
@@ -406,25 +447,29 @@
         heads, group = kv_heads // 2, query_heads // kv_heads
         qheads = heads * group
         pairs = group // PAIRS
-        q = jnp.transpose(queries, (1, 0, 2))
-        do = jnp.transpose(grad_out, (1, 0, 2))
-        kv = jnp.stack([jnp.transpose(keys, (1, 0, 2)), jnp.transpose(values, (1, 0, 2))], axis=1)
         bf16, f32 = jnp.bfloat16, jnp.float32
         vmem, dma = pltpu.VMEM, pltpu.SemaphoreType.DMA
         inside = pl.BlockSpec(memory_space=pltpu.VMEM)
+        outside = pl.BlockSpec(memory_space=pltpu.HBM)
 
         def body(*refs):
             kernel(heads, group, chips, blocks, *refs)
 
-        dq, dkv = pl.pallas_call(
+        return pl.pallas_call(
             body,
-            out_shape=[
-                jax.ShapeDtypeStruct((query_heads, tokens, dim), bf16),
-                jax.ShapeDtypeStruct((kv_heads, 2, tokens, dim), bf16),
-            ],
-            in_specs=[pl.BlockSpec(memory_space=pltpu.SMEM), inside, inside, inside],
-            out_specs=[inside, inside],
+            out_shape=[jax.ShapeDtypeStruct(each.shape, bf16) for each in (queries, keys, values)],
+            in_specs=[outside] * 5,
+            out_specs=[inside] * 3,
             scratch_shapes=[
+                pltpu.SMEM(doc_lengths.shape, jnp.int32),
+                vmem(queries.shape, bf16),
+                vmem(queries.shape, bf16),
+                vmem((2,) + keys.shape, bf16),
+                vmem((2, kv_heads, tokens, dim), bf16),
+                vmem((qheads, tokens, dim), bf16),
+                vmem((qheads, tokens, dim), bf16),
+                vmem((query_heads, tokens, dim), bf16),
+                vmem((2, kv_heads, tokens, dim), bf16),
                 vmem((heads, 2, WINDOW, dim), bf16),
                 vmem((2, qheads, tokens, dim), bf16),
                 vmem((2, qheads, tokens, dim), bf16),
@@ -449,15 +494,16 @@
                 dma((heads, pairs)),
                 dma((heads, 2)),
                 dma((heads, 2)),
+                dma((5,)),
             ],
             compiler_params=pltpu.CompilerParams(
                 collective_id=0, has_side_effects=True, vmem_limit_bytes=48 << 20
             ),
-        )(doc_lengths, q, do, kv)
-        return (
-            jnp.transpose(dq, (1, 0, 2)),
-            jnp.transpose(dkv[:, 0], (1, 0, 2)),
-            jnp.transpose(dkv[:, 1], (1, 0, 2)),
+        )(
+            *[
+                pltpu.with_memory_space_constraint(each, pltpu.HBM)
+                for each in (doc_lengths, queries, grad_out, keys, values)
+            ]
         )
 
     spread = P(("ctx", "uly"), None, None)

time: 80.4 us -> 73.2 us (0.910)
  local copies, waits for them, and re-layouts: 6.51 us -> 2.38 us
  Pallas kernels: 72.8 us -> 69.7 us
    pallas_call x1, Pallas kernels: 72.8 us -> 69.7 us  [local(): pl.pallas_call(body, out_shape=[jax.ShapeDtypeStruct(each.shape, bf16) fo...]
    unnamed x9 -> x3, local copies, waits for them, and re-layouts: 4.4 us -> 2.38 us
    another operation x1 -> x0, local copies, waits for them, and re-layouts: 1.27 us -> none  [local(): jnp.stack([jnp.transpose(keys, (1, 0, 2)), jnp.transpose(values, (1, 0, 2...]
    transpose x2 -> x0, local copies, waits for them, and re-layouts: 0.85 us -> none  [the longest x1 0.81 us: local(): do = jnp.transpose(grad_out, (1, 0, 2))]
where the time goes in v2:
time: 73.2 us; the launch traced here: 72.7 us
  Pallas kernels  69.7 us (95%)
  local copies, waits for them, and re-layouts  2.38 us (3%)
    pallas_call x1, Pallas kernels, local(): pl.pallas_call(body, out_shape=[jax.ShapeDtypeStruct(each.shape, bf16) fo...  69.7 us
    unnamed x3, local copies, waits for them, and re-layouts  2.38 us

profile of v2, /device:TPU:1, one launch (start us, length us, event | category | flops | bytes accessed | tf_op | source)
XLA Modules:
  0.0 72.7 jit_solution(3710287297248106628)
XLA Ops:
  0.6 69.7 %shard_map.76 = (bf16[128,32,128]{2,1,0:T(8,128)(2,1)S(1)}, bf16[128,8,128]{2,1,0:T(8,128)(2,1)S(1)}, bf16[128,8,128]{2,1,0:T(8,128)(2,1)S(1)}) custom-call(s32[64]{0:T(128)} %refs_0_.1, bf16[128,32,128]{2,1,0:T(8,128)(2,1)} %refs_1_.1, bf16[128,32,128]{2,1,0:T(8,128)(2,1)} %refs_2_.1, bf16[128,8,128]{2,1,0:T(8,128)(2,1)} %refs_3_.1, ...), custom_call_target="tpu_custom_call" | custom-call | tf_op jit(solution)/shard_map/pallas_call | solution.py:458
  70.3 1.0 %copy.11 = bf16[128,32,128]{2,1,0:T(8,128)(2,1)} copy(bf16[128,32,128]{2,1,0:T(8,128)(2,1)S(1)} %get-tuple-element.6) | data formatting | bytes 2097152
  71.3 0.7 copy.12
  72.0 0.7 copy.13

commit v3 on v2

--- a/solution.py
+++ b/solution.py
@@ -234,6 +234,7 @@
     def finish_head(h):
         for i in range(2):
             send_back(h, 0, i, 512, backward)
+        for i in range(2):
 
             @pl.when(core == 0)
             def _():
@@ -318,6 +319,9 @@
             for h in range(heads):
                 kvb[h, :, pl.ds(1024 + TOK * k, TOK), :] = kv_own[:, heads * k + h]
 
+    relay(0)
+    own_send(2)
+
     loads[4].wait()
     start_pos = chip * CHIP
     token = lax.broadcasted_iota(jnp.int32, (8, CHIP), 1) + start_pos
@@ -334,12 +338,6 @@
             key = lax.broadcasted_iota(jnp.int32, (TILE, TOK), 0) + tile * TILE
             bias[t, pl.ds(tile * TILE, TILE), :] = jnp.where((key >= low) & (key <= high), 0.0, -1e30)
 
-    for h in range(heads):
-        for n in range(2):
-            for tile in range(WINDOW // CHIP):
-                acc[h, n, pl.ds(tile * CHIP, CHIP), :] = jnp.zeros((CHIP, TOK), jnp.float32)
-    relay(0)
-    own_send(2)
     far_ready(1)
     all_ready(0)
 
@@ -393,8 +391,13 @@
             prob = s_scr[tile, :] * inverse
             dscore = (prob * (dp_scr[tile, :] - delta)).astype(jnp.bfloat16)
             dsb[tile, :] = dscore
-            acc[h, 1, key, :] += jnp.dot(prob.astype(jnp.bfloat16), do, preferred_element_type=jnp.float32)
-            acc[h, 0, key, :] += jnp.dot(dscore, q, preferred_element_type=jnp.float32)
+            terms = (
+                jnp.dot(dscore, q, preferred_element_type=jnp.float32),
+                jnp.dot(prob.astype(jnp.bfloat16), do, preferred_element_type=jnp.float32),
+            )
+            first = pair == 0 and (t == 0 or key.start >= SPAN)
+            for i in range(2):
+                acc[h, i, key, :] = terms[i] if first else acc[h, i, key, :] + terms[i]
         dq = lax.dot_general(dsb[...], kvb[h, 0, pl.ds(off, SPAN), :], TN, preferred_element_type=jnp.float32)
         dq = (dq * scale).astype(jnp.bfloat16).reshape(PAIRS, TOK, TOK)
 
@@ -438,6 +441,17 @@
     dv_out[...] = jnp.transpose(dkvh[1], (1, 0, 2))
 
 
+def put(dq, dk, dv, dq_out, dk_out, dv_out, sem):
+    copies = [
+        pltpu.make_async_copy(src, dst, sem.at[n])
+        for n, (src, dst) in enumerate(((dq, dq_out), (dk, dk_out), (dv, dv_out)))
+    ]
+    for copy in copies:
+        copy.start()
+    for copy in copies:
+        copy.wait()
+
+
 def solution(mesh):
     blocks, chips = mesh.shape["ctx"], mesh.shape["uly"] // 2
 
@@ -455,7 +469,7 @@
         def body(*refs):
             kernel(heads, group, chips, blocks, *refs)
 
-        return pl.pallas_call(
+        grads = pl.pallas_call(
             body,
             out_shape=[jax.ShapeDtypeStruct(each.shape, bf16) for each in (queries, keys, values)],
             in_specs=[outside] * 5,
@@ -505,6 +519,14 @@
                 for each in (doc_lengths, queries, grad_out, keys, values)
             ]
         )
+        return pl.pallas_call(
+            put,
+            out_shape=[jax.ShapeDtypeStruct(each.shape, bf16) for each in grads],
+            in_specs=[pl.BlockSpec(memory_space=pl.ANY)] * 3,
+            out_specs=[outside] * 3,
+            scratch_shapes=[dma((3,))],
+            compiler_params=pltpu.CompilerParams(vmem_limit_bytes=4 << 20),
+        )(*grads)
 
     spread = P(("ctx", "uly"), None, None)
     return jax.shard_map(

time: 73.2 us -> 71.2 us (0.973)
  local copies, waits for them, and re-layouts: 2.38 us -> 0 us
    unnamed x3 -> x0, local copies, waits for them, and re-layouts: 2.38 us -> none
    pallas_call x0 -> x1, Pallas kernels: none -> 1.16 us  [local(): pl.pallas_call(put, out_shape=[jax.ShapeDtypeStruct(each.shape, bf16) for...]
where the time goes in v3:
time: 71.2 us; the launch traced here: 71.1 us
  Pallas kernels  70.3 us (99%)
  between operations  0.82 us (1%)
    pallas_call x1, Pallas kernels, local(): pl.pallas_call(body, out_shape=[jax.ShapeDtypeStruct(each.shape, bf16) fo...  69.1 us

profile of v3, /device:TPU:1, one launch (start us, length us, event | category | flops | bytes accessed | tf_op | source)
XLA Modules:
  0.0 71.1 jit_solution(9605294955440381896)
XLA Ops:
  0.6 69.1 %shard_map.76 = (bf16[128,32,128]{2,1,0:T(8,128)(2,1)S(1)}, bf16[128,8,128]{2,1,0:T(8,128)(2,1)S(1)}, bf16[128,8,128]{2,1,0:T(8,128)(2,1)S(1)}) custom-call(s32[64]{0:T(128)} %refs_0_.1, bf16[128,32,128]{2,1,0:T(8,128)(2,1)} %refs_1_.1, bf16[128,32,128]{2,1,0:T(8,128)(2,1)} %refs_2_.1, bf16[128,8,128]{2,1,0:T(8,128)(2,1)} %refs_3_.1, ...), custom_call_target="tpu_custom_call" | custom-call | tf_op jit(solution)/shard_map/pallas_call | solution.py:472
  69.7 1.2 %shard_map.77 = (bf16[128,32,128]{2,1,0:T(8,128)(2,1)}, bf16[128,8,128]{2,1,0:T(8,128)(2,1)}, bf16[128,8,128]{2,1,0:T(8,128)(2,1)}) custom-call(bf16[128,32,128]{2,1,0:T(8,128)(2,1)S(1)} %get-tuple-element.6.dq, bf16[128,8,128]{2,1,0:T(8,128)(2,1)S(1)} %get-tuple-element.7.dk, bf16[128,8,128]{2,1,0:T(8,128)(2,1)S(1)} %get-tuple-element.8.dv), custom_call_target="tpu_custom_call" | custom-call | tf_op jit(solution)/shard_map/pallas_call | solution.py:522

commit v4 on v3

--- a/solution.py
+++ b/solution.py
@@ -231,9 +231,11 @@
         rows = pl.ds(pl.multiple_of(pos, 256), CHIP)
         acc[h, i, rows, :] = acc[h, i, rows, :] + rbuf[h, n, i].astype(jnp.float32)
 
-    def finish_head(h):
+    def two_back(h):
         for i in range(2):
             send_back(h, 0, i, 512, backward)
+
+    def one_back(h):
         for i in range(2):
 
             @pl.when(core == 0)
@@ -243,6 +245,10 @@
             @pl.when(core == 1)
             def _():
                 send_back(h, 1, i, 768, left())
+
+    def finish_head(h):
+        two_back(h)
+        one_back(h)
 
     def second_back(h):
         for i in range(2):
@@ -357,48 +363,68 @@
         15: [lambda: second_back(2)],
     }
 
-    for step in range(steps):
-        for each in hooks.get(step, ()):
-            each()
-        h = step // (2 * pairs)
-        t = step // pairs % 2
-        pair = step % pairs
-        off = t * TOK
+    stats = {}
+
+    def place_of(step):
+        return step // (2 * pairs), step // pairs % 2, step % pairs
+
+    def rows_of(step):
+        h, t, pair = place_of(step)
         mine = pl.ds(group * h + PAIRS * pair, PAIRS)
-        q = qv[t, mine].reshape(ROWS, TOK)
-        do = dov[t, mine].reshape(ROWS, TOK)
+        return qv[t, mine].reshape(ROWS, TOK), dov[t, mine].reshape(ROWS, TOK)
+
+    def weigh(step):
+        h, t, pair = place_of(step)
+        room = step % (2 * pairs)
+        q, do = rows_of(step)
         tiles = [pl.ds(tile * TILE, TILE) for tile in range(SPAN // TILE)]
-        keys = [pl.ds(off + tile * TILE, TILE) for tile in range(SPAN // TILE)]
         top = jnp.full((8, ROWS), -jnp.inf, jnp.float32)
-        for tile, key in zip(tiles, keys):
+        for tile in tiles:
+            key = pl.ds(t * TOK + tile.start, TILE)
             score = lax.dot_general(kvb[h, 0, key, :], q, NT, preferred_element_type=jnp.float32)
             score = score + jnp.concatenate([bias[t, tile, :]] * PAIRS, axis=1)
-            s_scr[tile, :] = score
-            dp_scr[tile, :] = lax.dot_general(kvb[h, 1, key, :], do, NT, preferred_element_type=jnp.float32)
+            s_scr[room, tile, :] = score
+            dp_scr[room, tile, :] = lax.dot_general(kvb[h, 1, key, :], do, NT, preferred_element_type=jnp.float32)
             top = jnp.maximum(top, jnp.max(score.reshape(TILE // 8, 8, ROWS), axis=0))
         factor = scale * LOG2E
         shift = jnp.max(top, axis=0, keepdims=True) * factor
         weight = jnp.zeros((8, ROWS), jnp.float32)
         weighted = jnp.zeros((8, ROWS), jnp.float32)
         for tile in tiles:
-            expo = jnp.exp2(s_scr[tile, :] * factor - shift)
-            s_scr[tile, :] = expo
+            expo = jnp.exp2(s_scr[room, tile, :] * factor - shift)
+            s_scr[room, tile, :] = expo
             weight = weight + jnp.sum(expo.reshape(TILE // 8, 8, ROWS), axis=0)
-            weighted = weighted + jnp.sum((expo * dp_scr[tile, :]).reshape(TILE // 8, 8, ROWS), axis=0)
+            weighted = weighted + jnp.sum((expo * dp_scr[room, tile, :]).reshape(TILE // 8, 8, ROWS), axis=0)
         inverse = 1.0 / jnp.sum(weight, axis=0, keepdims=True)
-        delta = jnp.sum(weighted, axis=0, keepdims=True) * inverse
-        for tile, key in zip(tiles, keys):
-            prob = s_scr[tile, :] * inverse
-            dscore = (prob * (dp_scr[tile, :] - delta)).astype(jnp.bfloat16)
-            dsb[tile, :] = dscore
+        stats[step] = inverse, jnp.sum(weighted, axis=0, keepdims=True) * inverse
+
+    def spread_terms(step, low=0, high=WINDOW):
+        h, t, pair = place_of(step)
+        room = step % (2 * pairs)
+        q, do = rows_of(step)
+        inverse, delta = stats[step]
+        for number in range(SPAN // TILE):
+            start = t * TOK + number * TILE
+            if not low <= start < high:
+                continue
+            tile, key = pl.ds(number * TILE, TILE), pl.ds(start, TILE)
+            prob = s_scr[room, tile, :] * inverse
+            dscore = (prob * (dp_scr[room, tile, :] - delta)).astype(jnp.bfloat16)
+            dsb[room, tile, :] = dscore
             terms = (
                 jnp.dot(dscore, q, preferred_element_type=jnp.float32),
                 jnp.dot(prob.astype(jnp.bfloat16), do, preferred_element_type=jnp.float32),
             )
-            first = pair == 0 and (t == 0 or key.start >= SPAN)
+            first = pair == 0 and (t == 0 or start >= SPAN)
             for i in range(2):
                 acc[h, i, key, :] = terms[i] if first else acc[h, i, key, :] + terms[i]
-        dq = lax.dot_general(dsb[...], kvb[h, 0, pl.ds(off, SPAN), :], TN, preferred_element_type=jnp.float32)
+
+    def query_terms(step):
+        h, t, pair = place_of(step)
+        room = step % (2 * pairs)
+        mine = pl.ds(group * h + PAIRS * pair, PAIRS)
+        keys = kvb[h, 0, pl.ds(t * TOK, SPAN), :]
+        dq = lax.dot_general(dsb[room], keys, TN, preferred_element_type=jnp.float32)
         dq = (dq * scale).astype(jnp.bfloat16).reshape(PAIRS, TOK, TOK)
 
         @pl.when(core == t)
@@ -410,9 +436,33 @@
             dqv[mine] = dq
             dq_swap(h, pair).start()
 
-    finish_head(3)
+    last = range(steps - 2 * pairs, steps)
+    for step in range(steps):
+        for each in hooks.get(step, ()):
+            each()
+        weigh(step)
+        if step not in last:
+            spread_terms(step)
+            query_terms(step)
+
+    def chunk_terms(pos):
+        for step in last:
+            spread_terms(step, pos, pos + CHIP)
+
+    chunk_terms(512)
+    two_back(3)
+    chunk_terms(256)
+    chunk_terms(768)
+    one_back(3)
     last_back(1)
+    chunk_terms(0)
     third_back(2)
+    chunk_terms(1024)
+    second_back(3)
+    for step in last:
+        query_terms(step)
+    last_back(2)
+    third_back(3)
     for h in range(heads):
         for pair in range(pairs):
             dq_swap(h, pair).wait_send()
@@ -420,9 +470,6 @@
     for k in (0, 1):
         some = pl.ds(qheads * k, qheads)
         dq_out[:, some, :] = jnp.transpose(dqh[some], (1, 0, 2))
-    second_back(3)
-    last_back(2)
-    third_back(3)
     last_back(3)
 
     for h in range(heads):
@@ -488,9 +535,9 @@
                 vmem((2, qheads, tokens, dim), bf16),
                 vmem((2, qheads, tokens, dim), bf16),
                 vmem((2, SPAN, TOK), f32),
-                vmem((SPAN, ROWS), f32),
-                vmem((SPAN, ROWS), f32),
-                vmem((SPAN, ROWS), bf16),
+                vmem((2 * pairs, SPAN, ROWS), f32),
+                vmem((2 * pairs, SPAN, ROWS), f32),
+                vmem((2 * pairs, SPAN, ROWS), bf16),
                 vmem((heads, 2, WINDOW, dim), f32),
                 vmem((qheads, tokens, dim), bf16),
                 vmem((heads, 4, 2, CHIP, dim), bf16),

time: 71.2 us -> 70.9 us (level)
  no operation moved by 1% of the time
where the time goes in v4:
time: 70.9 us; the launch traced here: 70.7 us
  Pallas kernels  69.9 us (99%)
  between operations  0.82 us (1%)
    pallas_call x1, Pallas kernels, local(): pl.pallas_call(body, out_shape=[jax.ShapeDtypeStruct(each.shape, bf16) fo...  68.8 us

profile of v4, /device:TPU:1, one launch (start us, length us, event | category | flops | bytes accessed | tf_op | source)
XLA Modules:
  0.0 70.7 jit_solution(11350063830145779471)
XLA Ops:
  0.6 68.8 %shard_map.76 = (bf16[128,32,128]{2,1,0:T(8,128)(2,1)S(1)}, bf16[128,8,128]{2,1,0:T(8,128)(2,1)S(1)}, bf16[128,8,128]{2,1,0:T(8,128)(2,1)S(1)}) custom-call(s32[64]{0:T(128)} %refs_0_.1, bf16[128,32,128]{2,1,0:T(8,128)(2,1)} %refs_1_.1, bf16[128,32,128]{2,1,0:T(8,128)(2,1)} %refs_2_.1, bf16[128,8,128]{2,1,0:T(8,128)(2,1)} %refs_3_.1, ...), custom_call_target="tpu_custom_call" | custom-call | tf_op jit(solution)/shard_map/pallas_call | solution.py:519
  69.4 1.2 %shard_map.77 = (bf16[128,32,128]{2,1,0:T(8,128)(2,1)}, bf16[128,8,128]{2,1,0:T(8,128)(2,1)}, bf16[128,8,128]{2,1,0:T(8,128)(2,1)}) custom-call(bf16[128,32,128]{2,1,0:T(8,128)(2,1)S(1)} %get-tuple-element.6.dq, bf16[128,8,128]{2,1,0:T(8,128)(2,1)S(1)} %get-tuple-element.7.dk, bf16[128,8,128]{2,1,0:T(8,128)(2,1)S(1)} %get-tuple-element.8.dv), custom_call_target="tpu_custom_call" | custom-call | tf_op jit(solution)/shard_map/pallas_call | solution.py:569

commit v5 on v4

--- a/solution.py
+++ b/solution.py
@@ -358,9 +358,8 @@
         10: [lambda: third_back(0)],
         11: [lambda: second_back(1)],
         12: [lambda: finish_head(2), lambda: all_ready(3)],
-        13: [lambda: last_back(0)],
-        14: [lambda: third_back(1)],
-        15: [lambda: second_back(2)],
+        14: [lambda: last_back(0)],
+        15: [lambda: third_back(1)],
     }
 
     stats = {}
@@ -451,13 +450,14 @@
 
     chunk_terms(512)
     two_back(3)
+    second_back(2)
     chunk_terms(256)
     chunk_terms(768)
     one_back(3)
+    chunk_terms(0)
     last_back(1)
-    chunk_terms(0)
+    chunk_terms(1024)
     third_back(2)
-    chunk_terms(1024)
     second_back(3)
     for step in last:
         query_terms(step)

time: 70.9 us -> 70.7 us (level)
  no operation moved by 1% of the time
where the time goes in v5:
time: 70.7 us; the launch traced here: 70.5 us
  Pallas kernels  69.7 us (99%)
  between operations  0.82 us (1%)
    pallas_call x1, Pallas kernels, local(): pl.pallas_call(body, out_shape=[jax.ShapeDtypeStruct(each.shape, bf16) fo...  68.5 us

profile of v5, /device:TPU:1, one launch (start us, length us, event | category | flops | bytes accessed | tf_op | source)
XLA Modules:
  0.0 70.5 jit_solution(5049302805652099448)
XLA Ops:
  0.6 68.5 %shard_map.76 = (bf16[128,32,128]{2,1,0:T(8,128)(2,1)S(1)}, bf16[128,8,128]{2,1,0:T(8,128)(2,1)S(1)}, bf16[128,8,128]{2,1,0:T(8,128)(2,1)S(1)}) custom-call(s32[64]{0:T(128)} %refs_0_.1, bf16[128,32,128]{2,1,0:T(8,128)(2,1)} %refs_1_.1, bf16[128,32,128]{2,1,0:T(8,128)(2,1)} %refs_2_.1, bf16[128,8,128]{2,1,0:T(8,128)(2,1)} %refs_3_.1, ...), custom_call_target="tpu_custom_call" | custom-call | tf_op jit(solution)/shard_map/pallas_call | solution.py:519
  69.2 1.2 %shard_map.77 = (bf16[128,32,128]{2,1,0:T(8,128)(2,1)}, bf16[128,8,128]{2,1,0:T(8,128)(2,1)}, bf16[128,8,128]{2,1,0:T(8,128)(2,1)}) custom-call(bf16[128,32,128]{2,1,0:T(8,128)(2,1)S(1)} %get-tuple-element.6.dq, bf16[128,8,128]{2,1,0:T(8,128)(2,1)S(1)} %get-tuple-element.7.dk, bf16[128,8,128]{2,1,0:T(8,128)(2,1)S(1)} %get-tuple-element.8.dv), custom_call_target="tpu_custom_call" | custom-call | tf_op jit(solution)/shard_map/pallas_call | solution.py:569
